TPU v7x, 256 devices: a whole 4x4x8 slice. The times are simulated.
256 devices in a mesh: row: 4 (over x_lo, core), col: 64 (over y, x_hi, z).
Axes of the slice: x: 4 (x_hi: 2, x_lo: 2; x = x_hi * 2 + x_lo), y: 4, z: 8, core: 2. Of those that a mesh axis runs over, the one named last changes fastest.
Arguments:
- test_points: float32 [3, 4096], P(None, ('row', 'col')), may hold values from 0 to 1
- src_points: float32 [3, 262144], P(None, ('row', 'col')), may hold values from 0 to 1
- currents: float32 [2, 262144], P(None, ('row', 'col')), may hold values from -6 to 6
- near_blocks: float32 [16384, 2, 16, 128], P(('row', 'col')), may hold values from -0.3 to 0.3
- near_dest: int32 [16384, 1], P(('row', 'col')), may hold values from 0 to 63; in each aligned block of 64 rows (0 to 63, 64 to 127, ...) at most 2 rows name the same one
- near_tile: int32 [16384, 1], P(('row', 'col')), may hold values from 0 to 7
Outputs:
- field: float32 [2, 4096], P(None, ('row', 'col'))
Inputs may be any that keep to these rules, and one draw needn't show every extreme that they name: `near_dest`: among the 64 blocks held by one device, at most 2 name the same column index; some device reaches 2 in every draw.
All inputs are finite; a program needn't handle non-finite values.
Results may differ from a plain program's by a relative error of at most 0.0003.
Values sent between devices are 32-bit elements; how exact they have to be, the bound alone decides.
A program may use at most 64 MiB of HBM per device.

v0:
```python
import math
import jax
import jax.numpy as jnp
from jax import lax
from jax.sharding import PartitionSpec as P

CAP = 2
WAVENUMBER = 40.0
SOFTENING = 0.01


def far_terms(targets, sources, current):
    row_count = targets.shape[1]
    src_width = sources.shape[1]
    entry_limit = max(128, (1 << 20) // row_count)
    stride = math.gcd(src_width, 1 << entry_limit.bit_length() - 1)
    blocks = src_width // stride
    source_blocks = sources.reshape(3, blocks, stride).transpose(1, 0, 2)
    current_blocks = current.reshape(2, blocks, stride).transpose(1, 0, 2)

    def accumulate(running, block_pair):
        points, values = block_pair
        delta_x = targets[0][:, None] - points[0][None, :]
        delta_y = targets[1][:, None] - points[1][None, :]
        delta_z = targets[2][:, None] - points[2][None, :]
        distance = jnp.sqrt(
            delta_x * delta_x + delta_y * delta_y + delta_z * delta_z + SOFTENING * SOFTENING
        )
        phases = WAVENUMBER * distance
        kernel_re = jnp.cos(phases) / distance
        kernel_im = -jnp.sin(phases) / distance
        real_part = jnp.sum(kernel_re * values[0][None, :] - kernel_im * values[1][None, :], axis=1)
        imag_part = jnp.sum(kernel_re * values[1][None, :] + kernel_im * values[0][None, :], axis=1)
        return (running + jnp.stack([real_part, imag_part]), None)

    running, _ = lax.scan(
        accumulate, jnp.zeros((2, row_count), jnp.float32), (source_blocks, current_blocks)
    )
    return running


def far_part(test_points, src_points, currents):
    block_src, block_cur = (
        lax.all_gather(src_points, "row", axis=1, tiled=True),
        lax.all_gather(currents, "row", axis=1, tiled=True),
    )
    return far_terms(
        test_points,
        lax.all_gather(block_src, "col", axis=1, tiled=True),
        lax.all_gather(block_cur, "col", axis=1, tiled=True),
    )


def near_part(currents, near_blocks, near_dest, near_tile):
    items = near_blocks.shape[0]
    row_dev = near_blocks.shape[2]
    tile_width = near_blocks.shape[3]
    columns = lax.axis_size("col")
    tile_count = currents.shape[1] // tile_width
    highest = lax.Precision.HIGHEST
    tile_ids = near_tile[:, 0]
    target_col = near_dest[:, 0]
    picker = (tile_ids[:, None] == jnp.arange(tile_count, dtype=jnp.int32)[None, :]).astype(
        jnp.float32
    )
    chosen = jnp.einsum(
        "kt,ctj->kcj", picker, currents.reshape(2, tile_count, tile_width), precision=highest
    )
    blocks_re = near_blocks[:, 0]
    blocks_im = near_blocks[:, 1]
    term_re = jnp.einsum("kij,kj->ki", blocks_re, chosen[:, 0], precision=highest) - jnp.einsum(
        "kij,kj->ki", blocks_im, chosen[:, 1], precision=highest
    )
    term_im = jnp.einsum("kij,kj->ki", blocks_re, chosen[:, 1], precision=highest) + jnp.einsum(
        "kij,kj->ki", blocks_im, chosen[:, 0], precision=highest
    )
    terms = jnp.concatenate([term_re, term_im], axis=1)
    positions = jnp.arange(items, dtype=jnp.int32)
    earlier = (target_col[:, None] == target_col[None, :]) & (
        positions[None, :] < positions[:, None]
    )
    ranking = jnp.sum(earlier.astype(jnp.int32), axis=1)
    slot_ids = target_col * CAP + ranking
    placer = (slot_ids[:, None] == jnp.arange(columns * CAP, dtype=jnp.int32)[None, :]).astype(
        jnp.float32
    )
    outgoing = jnp.einsum("ks,kf->sf", placer, terms, precision=highest).reshape(
        columns, CAP * 2 * row_dev
    )
    incoming = lax.all_to_all(outgoing, "col", split_axis=0, concat_axis=0, tiled=True)
    return incoming.reshape(columns * CAP, 2, row_dev).sum(axis=0)


def local(test_points, src_points, currents, near_blocks, near_dest, near_tile):
    total_sources = src_points.shape[1] * lax.axis_size("row") * lax.axis_size("col")
    factor = 1.0 / math.sqrt(total_sources)
    far = far_part(test_points, src_points, currents)
    near = near_part(currents, near_blocks, near_dest, near_tile)
    return far * factor + near


def solution(mesh):
    in_specs = (
        P(None, ("row", "col")),
        P(None, ("row", "col")),
        P(None, ("row", "col")),
        P(("row", "col"), None, None, None),
        P(("row", "col"), None),
        P(("row", "col"), None),
    )
    out_specs = P(None, ("row", "col"))
    return jax.shard_map(local, mesh=mesh, in_specs=in_specs, out_specs=out_specs, check_vma=False)
```

profile of v0, /device:TPU:8, one launch (start us, length us, event | category | flops | bytes accessed | tf_op | source)
XLA Modules:
  0.0 363.5 jit_solution(17013263100812028713)
XLA Ops:
  6.5 0.0 all-gather.5.cloned.1.call-start
  6.5 6.6 %all_gather.14 = f32[2,4096]{1,0:T(2,128)} all-gather(f32[2,1024]{1,0:T(2,128)} %param.10), channel_id=1, replica_groups=mesh['row'=4,'col'=64] {'row'}, dimensions={1}, use_global_device_ids=true | all-gather | bytes 40960 | tf_op jit(solution)/shard_map/all_gather | solution.py:45
  13.1 0.0 all-gather.5.cloned.1.call-update
  13.1 0.0 all-gather.3.cloned.1.call-start
  13.2 5.9 %all_gather.12 = f32[3,4096]{1,0:T(4,128)} all-gather(f32[3,1024]{1,0:T(4,128)} %param.9), channel_id=1, replica_groups=mesh['row'=4,'col'=64] {'row'}, dimensions={1}, use_global_device_ids=true | all-gather | bytes 61440 | tf_op jit(solution)/shard_map/all_gather | solution.py:44
  19.1 0.0 all-gather.3.cloned.1.call-update
  19.1 0.9 fusion.18
  20.1 2.0 fusion.6
  22.1 2.0 fusion.2
  24.1 2.0 fusion.4
  26.1 2.0 fusion
  28.1 0.9 convert_reduce_fusion
  29.0 0.7 fusion.24
  29.7 0.3 fusion.12
  30.0 0.7 all_to_all.6
  30.7 14.4 %all-to-all-start = ((f32[64,1,64]{2,1,0:T(1,128)}), f32[64,1,64]{2,1,0:T(1,128)S(1)}, u32[]{:S(2)}, u32[]{:S(2)}) async-start(f32[64,1,64]{2,1,0:T(1,128)} %bitcast.27), calls=%async_computation | async-start | bytes 65536 | tf_op jit(solution)/shard_map/all_to_all | solution.py:90
  45.0 10.8 %all-to-all-done = f32[64,1,64]{2,1,0:T(1,128)S(1)} async-done(((f32[64,1,64]{2,1,0:T(1,128)}), f32[64,1,64]{2,1,0:T(1,128)S(1)}, u32[]{:S(2)}, u32[]{:S(2)}) %all-to-all-start) | async-done | bytes 16416 | tf_op jit(solution)/shard_map/all_to_all | solution.py:90
  55.8 0.5 broadcast.38
  56.3 0.7 reduce.3
  57.1 0.1 reshape.35
  57.2 0.1 reduce_sum.40
  57.4 77.2 %all-gather.5.cloned.1.call-done = f32[2,262144]{1,0:T(2,128)} async-done(((f32[2,4096]{1,0:T(2,128)}), f32[2,262144]{1,0:T(2,128)}) %all-gather.5.cloned.1.call-update) | async-done | bytes 2097168 | tf_op jit(solution)/shard_map/all_gather | solution.py:50
  134.6 127.7 %all-gather.3.cloned.1.call-done = f32[3,262144]{1,0:T(4,128)} async-done(((f32[3,4096]{1,0:T(4,128)}), f32[3,262144]{1,0:T(4,128)}) %all-gather.3.cloned.1.call-update) | async-done | bytes 3145744 | tf_op jit(solution)/shard_map/all_gather | solution.py:49
  262.3 93.8 %while.11 = (s32[]{:T(128)}, f32[2,16]{1,0:T(2,128)S(1)}, f32[3,16]{1,0:T(4,128)}, f32[4,3,65536]{2,1,0:T(4,128)}, f32[4,2,65536]{2,1,0:T(2,128)}, /*index=5*/s32[]{:T(128)}, s32[]{:T(128)}, s32[]{}, s32[]{}) while((s32[]{:T(128)}, f32[2,16]{1,0:T(2,128)S(1)}, f32[3,16]{1,0:T(4,128)}, f32[4,3,65536]{2,1,0:T(4,128)}, ...), condition=%wide.region_3.4_spmd.clone, body=%wide.region_0.3_spmd.clone.sunk | while | flops 22020164 | bytes 3933387 | solution.py:36
  262.3 3.4 constant_dynamic-slice_fusion.6
  265.7 0.8 slice_bitcast_fusion.4
  266.5 19.1 %subtract_reduce_fusion.2 = (f32[16]{0:T(128)S(1)}, f32[16]{0:T(128)S(1)}) fusion(f32[65536]{0:T(1024)S(1)} %bitcast.82, f32[65536]{0:T(1024)S(1)} %bitcast.81, f32[65536]{0:T(1024)S(1)} %bitcast.83, f32[16]{0:T(128)S(1)} %get-tuple-element.120, f32[65536]{0:T(1024)S(1)} %bitcast.84, f32[16]{0:T(128)S(1)} %get-tuple-element.122, ...), kind=kLoop, calls=%fused_computation.1.clone.1 | loop fusion | flops 22020064 | bytes 1311040 | tf_op jit(solution)/shard_map/while/body/eval_jaxpr/reduce_sum | solution.py:32
  285.6 3.7 %constant_dynamic-slice_fusion.6 = (f32[1,1,65536]{2,1,0:T(1,128)S(1)}, f32[1,1,65536]{2,1,0:T(1,128)S(1)}, f32[1,1,65536]{2,1,0:T(1,128)S(1)}, f32[1,1,65536]{2,1,0:T(1,128)S(1)}, f32[1,1,65536]{2,1,0:T(1,128)S(1)}) fusion(f32[4,2,65536]{2,1,0:T(2,128)} %get-tuple-element.149, s32[]{:T(128)} %get-tuple-element.136, s32[]{:T(128)S(6)} %add.101, ...), kind=kLoop, calls=%fused_computation.5.clone.1 | loop fusion | bytes 2621452 | tf_op jit(solution)/shard_map/while/body/eval_jaxpr/slice | solution.py:32
  289.3 0.8 slice_bitcast_fusion.4
  290.1 19.1 %subtract_reduce_fusion.2 = (f32[16]{0:T(128)S(1)}, f32[16]{0:T(128)S(1)}) fusion(f32[65536]{0:T(1024)S(1)} %bitcast.82, f32[65536]{0:T(1024)S(1)} %bitcast.81, f32[65536]{0:T(1024)S(1)} %bitcast.83, f32[16]{0:T(128)S(1)} %get-tuple-element.120, f32[65536]{0:T(1024)S(1)} %bitcast.84, f32[16]{0:T(128)S(1)} %get-tuple-element.122, ...), kind=kLoop, calls=%fused_computation.1.clone.1 | loop fusion | flops 22020064 | bytes 1311040 | tf_op jit(solution)/shard_map/while/body/eval_jaxpr/reduce_sum | solution.py:32
  309.2 3.5 constant_dynamic-slice_fusion.6
  312.7 0.8 slice_bitcast_fusion.4
  313.5 19.1 %subtract_reduce_fusion.2 = (f32[16]{0:T(128)S(1)}, f32[16]{0:T(128)S(1)}) fusion(f32[65536]{0:T(1024)S(1)} %bitcast.82, f32[65536]{0:T(1024)S(1)} %bitcast.81, f32[65536]{0:T(1024)S(1)} %bitcast.83, f32[16]{0:T(128)S(1)} %get-tuple-element.120, f32[65536]{0:T(1024)S(1)} %bitcast.84, f32[16]{0:T(128)S(1)} %get-tuple-element.122, ...), kind=kLoop, calls=%fused_computation.1.clone.1 | loop fusion | flops 22020064 | bytes 1311040 | tf_op jit(solution)/shard_map/while/body/eval_jaxpr/reduce_sum | solution.py:32
  332.7 3.6 constant_dynamic-slice_fusion.6
  336.2 0.8 slice_bitcast_fusion.4
  337.0 19.1 %subtract_reduce_fusion.2 = (f32[16]{0:T(128)S(1)}, f32[16]{0:T(128)S(1)}) fusion(f32[65536]{0:T(1024)S(1)} %bitcast.82, f32[65536]{0:T(1024)S(1)} %bitcast.81, f32[65536]{0:T(1024)S(1)} %bitcast.83, f32[16]{0:T(128)S(1)} %get-tuple-element.120, f32[65536]{0:T(1024)S(1)} %bitcast.84, f32[16]{0:T(128)S(1)} %get-tuple-element.122, ...), kind=kLoop, calls=%fused_computation.1.clone.1 | loop fusion | flops 22020064 | bytes 1311040 | tf_op jit(solution)/shard_map/while/body/eval_jaxpr/reduce_sum | solution.py:32
  356.1 0.6 multiply_add_fusion
  (8 shorter events, 0.1 us)
Async XLA Ops:
  6.5 128.1 %all-gather.5.cloned.1.call-start = ((), (), s32[]{:S(2)}) async-start(), calls=%async_computation.2 | async-start | bytes 2129920 | tf_op jit(solution)/shard_map/all_gather | solution.py:50
  13.1 249.2 %all-gather.3.cloned.1.call-start = ((), (), s32[]{:S(2)}) async-start(), calls=%async_computation.1 | async-start | bytes 4259840 | tf_op jit(solution)/shard_map/all_gather | solution.py:49
  30.7 25.2 %all-to-all-start = ((f32[64,1,64]{2,1,0:T(1,128)}), f32[64,1,64]{2,1,0:T(1,128)S(1)}, u32[]{:S(2)}, u32[]{:S(2)}) async-start(f32[64,1,64]{2,1,0:T(1,128)} %bitcast.27), calls=%async_computation | async-start | bytes 65536 | tf_op jit(solution)/shard_map/all_to_all | solution.py:90
Sparse Core Ops, SparseCore 0:
  13.3 121.3 all-gather.4
  138.1 124.1 all-gather.2
where the time goes:
time: 364 us
  waiting for transfers between devices  216 us (59%)
  other arithmetic  79.4 us (22%)
  local copies, waits for them, and re-layouts  18.7 us (5%)
  starting transfers between devices  14.4 us (4%)
  between operations  13.5 us (4%)
  blocking collectives  12.5 us (3%)
  matrix products  9.2 us (3%)
    all_gather x1, waiting for transfers between devices, far_part(): lax.all_gather(block_src, 'col', axis=1, tiled=True)  128 us
    all_gather x1, waiting for transfers between devices, far_part(): lax.all_gather(block_cur, 'col', axis=1, tiled=True)  77.2 us
    reduce_sum x4, other arithmetic, accumulate(): jnp.sum(kernel_re * values[0][None, :] - kernel_im * values[1][None, :],...  76.3 us
    all_to_all x1, starting transfers between devices, near_part(): lax.all_to_all(outgoing, 'col', split_axis=0, concat_axis=0, tiled=True)  14.4 us
    slice x4, local copies, waits for them, and re-layouts, accumulate(): values[0][None, :]  14.1 us
    all_to_all x1, waiting for transfers between devices, near_part(): lax.all_to_all(outgoing, 'col', split_axis=0, concat_axis=0, tiled=True)  10.8 us
  transfers between devices with their start and end apart: 3, of which 3 were waited for; matrix products, arithmetic and copies ran while one was open for 3% of the time, Pallas kernels for 0%

commit v1 on v0

--- a/solution.py
+++ b/solution.py
@@ -46,7 +46,9 @@
     )
     return far_terms(
         test_points,
-        lax.all_gather(block_src, "col", axis=1, tiled=True),
+        jnp.concatenate(
+            lax.all_to_all(jnp.stack([block_src] * lax.axis_size("col")), "col", 0, 0), axis=1
+        ),
         lax.all_gather(block_cur, "col", axis=1, tiled=True),
     )
 

time: 364 us -> 294 us (0.81)
  waiting for transfers between devices: 216 us -> 133 us
  starting transfers between devices: 14.4 us -> 22.2 us
  blocking collectives: 12.5 us -> 17.2 us
    all_gather x1 -> x0, waiting for transfers between devices: 128 us -> none  [far_part(): lax.all_gather(block_src, 'col', axis=1, tiled=True)]
    all_gather x1, waiting for transfers between devices: 77.2 us -> 128 us  [far_part(): lax.all_gather(block_cur, 'col', axis=1, tiled=True)]
    all_to_all x0 -> x1, starting transfers between devices: none -> 7.58 us  [far_part(): lax.all_to_all(jnp.stack([block_src] * lax.axis_size('col')), 'col', 0, 0)]
    all_to_all x1, waiting for transfers between devices: 10.8 us -> 5.49 us  [near_part(): lax.all_to_all(outgoing, 'col', split_axis=0, concat_axis=0, tiled=True)]
    all_gather x1, blocking collectives: 6.57 us -> 11.7 us  [far_part(): lax.all_gather(currents, 'row', axis=1, tiled=True)]
  transfers between devices with their start and end apart: 3 -> 3, of which waited for: 3 -> 2; matrix products, arithmetic and copies ran while one was open for 3% -> 1% of each run, Pallas kernels for 0% -> 0%
where the time goes in v1:
time: 294 us; the launch traced here: 293 us
  waiting for transfers between devices  133 us (45%)
  other arithmetic  79.5 us (27%)
  starting transfers between devices  22.2 us (8%)
  local copies, waits for them, and re-layouts  18.4 us (6%)
  blocking collectives  17.2 us (6%)
  between operations  13.5 us (5%)
  matrix products  9.2 us (3%)
    all_gather x1, waiting for transfers between devices, far_part(): lax.all_gather(block_cur, 'col', axis=1, tiled=True)  128 us
    reduce_sum x4, other arithmetic, accumulate(): jnp.sum(kernel_re * values[0][None, :] - kernel_im * values[1][None, :],...  76.4 us
    all_to_all x1, starting transfers between devices, near_part(): lax.all_to_all(outgoing, 'col', split_axis=0, concat_axis=0, tiled=True)  14.6 us
    slice x4, local copies, waits for them, and re-layouts, accumulate(): values[0][None, :]  14 us
    all_gather x1, blocking collectives, far_part(): lax.all_gather(currents, 'row', axis=1, tiled=True)  11.7 us
    all_to_all x1, starting transfers between devices, far_part(): lax.all_to_all(jnp.stack([block_src] * lax.axis_size('col')), 'col', 0, 0)  7.58 us
  transfers between devices with their start and end apart: 3, of which 2 were waited for; matrix products, arithmetic and copies ran while one was open for 1% of the time, Pallas kernels for 0%

profile of v1, /device:TPU:8, one launch (start us, length us, event | category | flops | bytes accessed | tf_op | source)
XLA Modules:
  0.0 293.1 jit_solution(14032323530267376620)
XLA Ops:
  6.5 0.9 fusion.18
  7.5 2.0 fusion.2
  9.5 2.0 fusion.4
  11.5 2.0 fusion.6
  13.5 2.0 fusion
  15.5 0.9 convert_reduce_fusion
  16.4 0.7 fusion.24
  17.0 0.3 fusion.12
  17.4 0.7 all_to_all.10
  18.0 14.6 %all-to-all-start.1 = ((f32[64,1,64]{2,1,0:T(1,128)}), f32[64,1,64]{2,1,0:T(1,128)S(1)}, u32[]{:S(2)}, u32[]{:S(2)}) async-start(f32[64,1,64]{2,1,0:T(1,128)} %bitcast.28), calls=%async_computation.1 | async-start | bytes 65536 | tf_op jit(solution)/shard_map/all_to_all | solution.py:92
  32.6 5.5 %all_gather.9 = f32[3,4096]{1,0:T(4,128)S(1)} all-gather(f32[3,1024]{1,0:T(4,128)} %param.9), channel_id=1, replica_groups=mesh['row'=4,'col'=64] {'row'}, dimensions={1}, use_global_device_ids=true | all-gather | bytes 61440 | tf_op jit(solution)/shard_map/all_gather | solution.py:44
  38.1 5.5 %all-to-all-done.1 = f32[64,1,64]{2,1,0:T(1,128)S(1)} async-done(((f32[64,1,64]{2,1,0:T(1,128)}), f32[64,1,64]{2,1,0:T(1,128)S(1)}, u32[]{:S(2)}, u32[]{:S(2)}) %all-to-all-start.1) | async-done | bytes 16416 | tf_op jit(solution)/shard_map/all_to_all | solution.py:92
  43.6 3.0 %stack.8 = f32[64,3,4096]{2,1,0:T(4,128)} broadcast(f32[3,4096]{1,0:T(4,128)S(1)} %all_gather.9), dimensions={1,2} | broadcast | bytes 3194880 | tf_op jit(solution)/shard_map/stack | solution.py:50
  46.6 0.0 copy-start
  46.6 0.0 copy-start.1
  46.6 7.6 %all-to-all-start = ((f32[64,3,4096]{2,1,0:T(4,128)}), f32[64,3,4096]{2,1,0:T(4,128)}, u32[]{:S(2)}, u32[]{:S(2)}) async-start(f32[64,3,4096]{2,1,0:T(4,128)} %stack.8), calls=%async_computation | async-start | bytes 8388608 | tf_op jit(solution)/shard_map/all_to_all | solution.py:50
  54.1 0.0 all-gather.2.cloned.1.call-start
  54.2 0.0 copy-done
  54.2 11.7 %all_gather.10 = f32[2,4096]{1,0:T(2,128)} all-gather(f32[2,1024]{1,0:T(2,128)S(1)} %copy-done), channel_id=1, replica_groups=mesh['row'=4,'col'=64] {'row'}, dimensions={1}, use_global_device_ids=true | all-gather | bytes 40960 | tf_op jit(solution)/shard_map/all_gather | solution.py:45
  65.9 0.0 all-gather.2.cloned.1.call-update
  65.9 0.5 broadcast.40
  66.5 0.7 reduce.3
  67.2 0.1 reshape.37
  67.4 0.1 reduce_sum.40
  67.5 127.6 %all-gather.2.cloned.1.call-done = f32[2,262144]{1,0:T(2,128)} async-done(((f32[2,4096]{1,0:T(2,128)}), f32[2,262144]{1,0:T(2,128)}) %all-gather.2.cloned.1.call-update) | async-done | bytes 2097168 | tf_op jit(solution)/shard_map/all_gather | solution.py:52
  195.1 0.0 all-to-all-done
  195.1 0.0 copy-done.1
  195.1 90.6 %while.11 = (s32[]{:T(128)}, f32[2,16]{1,0:T(2,128)S(1)}, f32[3,16]{1,0:T(4,128)S(1)}, f32[4,3,65536]{2,1,0:T(4,128)}, f32[4,2,65536]{2,1,0:T(2,128)}, /*index=5*/s32[]{:T(128)}, s32[]{:T(128)}, s32[]{}, s32[]{}) while((s32[]{:T(128)}, f32[2,16]{1,0:T(2,128)S(1)}, f32[3,16]{1,0:T(4,128)S(1)}, f32[4,3,65536]{2,1,0:T(4,128)}, ...), condition=%wide.region_3.4_spmd.clone, body=%wide.region_0.3_spmd.clone.sunk | while | flops 22020164 | bytes 3933387 | solution.py:36
  195.1 3.4 %constant_dynamic-slice_fusion.6 = (f32[1,1,65536]{2,1,0:T(1,128)S(1)}, f32[1,1,65536]{2,1,0:T(1,128)S(1)}, f32[1,1,65536]{2,1,0:T(1,128)S(1)}, f32[1,1,65536]{2,1,0:T(1,128)S(1)}, f32[1,1,65536]{2,1,0:T(1,128)S(1)}) fusion(f32[4,2,65536]{2,1,0:T(2,128)} %get-tuple-element.149, s32[]{:T(128)} %get-tuple-element.136, s32[]{:T(128)S(6)} %add.101, ...), kind=kLoop, calls=%fused_computation.5.clone.1 | loop fusion | bytes 2621452 | tf_op jit(solution)/shard_map/while/body/eval_jaxpr/slice | solution.py:32
  198.5 19.1 %subtract_reduce_fusion.2 = (f32[16]{0:T(128)S(1)}, f32[16]{0:T(128)S(1)}) fusion(f32[65536]{0:T(1024)S(1)} %bitcast.84, f32[65536]{0:T(1024)S(1)} %bitcast.83, f32[65536]{0:T(1024)S(1)} %bitcast.85, f32[16]{0:T(128)S(1)} %get-tuple-element.120, f32[65536]{0:T(1024)S(1)} %bitcast.86, f32[16]{0:T(128)S(1)} %get-tuple-element.122, ...), kind=kLoop, calls=%fused_computation.1.clone.1 | loop fusion | flops 22020064 | bytes 1311040 | tf_op jit(solution)/shard_map/while/body/eval_jaxpr/reduce_sum | solution.py:32
  217.6 3.6 %constant_dynamic-slice_fusion.6 = (f32[1,1,65536]{2,1,0:T(1,128)S(1)}, f32[1,1,65536]{2,1,0:T(1,128)S(1)}, f32[1,1,65536]{2,1,0:T(1,128)S(1)}, f32[1,1,65536]{2,1,0:T(1,128)S(1)}, f32[1,1,65536]{2,1,0:T(1,128)S(1)}) fusion(f32[4,2,65536]{2,1,0:T(2,128)} %get-tuple-element.149, s32[]{:T(128)} %get-tuple-element.136, s32[]{:T(128)S(6)} %add.101, ...), kind=kLoop, calls=%fused_computation.5.clone.1 | loop fusion | bytes 2621452 | tf_op jit(solution)/shard_map/while/body/eval_jaxpr/slice | solution.py:32
  221.2 19.1 %subtract_reduce_fusion.2 = (f32[16]{0:T(128)S(1)}, f32[16]{0:T(128)S(1)}) fusion(f32[65536]{0:T(1024)S(1)} %bitcast.84, f32[65536]{0:T(1024)S(1)} %bitcast.83, f32[65536]{0:T(1024)S(1)} %bitcast.85, f32[16]{0:T(128)S(1)} %get-tuple-element.120, f32[65536]{0:T(1024)S(1)} %bitcast.86, f32[16]{0:T(128)S(1)} %get-tuple-element.122, ...), kind=kLoop, calls=%fused_computation.1.clone.1 | loop fusion | flops 22020064 | bytes 1311040 | tf_op jit(solution)/shard_map/while/body/eval_jaxpr/reduce_sum | solution.py:32
  240.4 3.5 %constant_dynamic-slice_fusion.6 = (f32[1,1,65536]{2,1,0:T(1,128)S(1)}, f32[1,1,65536]{2,1,0:T(1,128)S(1)}, f32[1,1,65536]{2,1,0:T(1,128)S(1)}, f32[1,1,65536]{2,1,0:T(1,128)S(1)}, f32[1,1,65536]{2,1,0:T(1,128)S(1)}) fusion(f32[4,2,65536]{2,1,0:T(2,128)} %get-tuple-element.149, s32[]{:T(128)} %get-tuple-element.136, s32[]{:T(128)S(6)} %add.101, ...), kind=kLoop, calls=%fused_computation.5.clone.1 | loop fusion | bytes 2621452 | tf_op jit(solution)/shard_map/while/body/eval_jaxpr/slice | solution.py:32
  243.9 19.1 %subtract_reduce_fusion.2 = (f32[16]{0:T(128)S(1)}, f32[16]{0:T(128)S(1)}) fusion(f32[65536]{0:T(1024)S(1)} %bitcast.84, f32[65536]{0:T(1024)S(1)} %bitcast.83, f32[65536]{0:T(1024)S(1)} %bitcast.85, f32[16]{0:T(128)S(1)} %get-tuple-element.120, f32[65536]{0:T(1024)S(1)} %bitcast.86, f32[16]{0:T(128)S(1)} %get-tuple-element.122, ...), kind=kLoop, calls=%fused_computation.1.clone.1 | loop fusion | flops 22020064 | bytes 1311040 | tf_op jit(solution)/shard_map/while/body/eval_jaxpr/reduce_sum | solution.py:32
  263.1 3.5 %constant_dynamic-slice_fusion.6 = (f32[1,1,65536]{2,1,0:T(1,128)S(1)}, f32[1,1,65536]{2,1,0:T(1,128)S(1)}, f32[1,1,65536]{2,1,0:T(1,128)S(1)}, f32[1,1,65536]{2,1,0:T(1,128)S(1)}, f32[1,1,65536]{2,1,0:T(1,128)S(1)}) fusion(f32[4,2,65536]{2,1,0:T(2,128)} %get-tuple-element.149, s32[]{:T(128)} %get-tuple-element.136, s32[]{:T(128)S(6)} %add.101, ...), kind=kLoop, calls=%fused_computation.5.clone.1 | loop fusion | bytes 2621452 | tf_op jit(solution)/shard_map/while/body/eval_jaxpr/slice | solution.py:32
  266.6 19.1 %subtract_reduce_fusion.2 = (f32[16]{0:T(128)S(1)}, f32[16]{0:T(128)S(1)}) fusion(f32[65536]{0:T(1024)S(1)} %bitcast.84, f32[65536]{0:T(1024)S(1)} %bitcast.83, f32[65536]{0:T(1024)S(1)} %bitcast.85, f32[16]{0:T(128)S(1)} %get-tuple-element.120, f32[65536]{0:T(1024)S(1)} %bitcast.86, f32[16]{0:T(128)S(1)} %get-tuple-element.122, ...), kind=kLoop, calls=%fused_computation.1.clone.1 | loop fusion | flops 22020064 | bytes 1311040 | tf_op jit(solution)/shard_map/while/body/eval_jaxpr/reduce_sum | solution.py:32
  285.7 0.6 multiply_add_fusion
  (12 shorter events, 0.1 us)
Async XLA Ops:
  18.0 25.5 %all-to-all-start.1 = ((f32[64,1,64]{2,1,0:T(1,128)}), f32[64,1,64]{2,1,0:T(1,128)S(1)}, u32[]{:S(2)}, u32[]{:S(2)}) async-start(f32[64,1,64]{2,1,0:T(1,128)} %bitcast.28), calls=%async_computation.1 | async-start | bytes 65536 | tf_op jit(solution)/shard_map/all_to_all | solution.py:92
  46.6 7.6 %copy-start = (f32[2,1024]{1,0:T(2,128)S(1)}, f32[2,1024]{1,0:T(2,128)}, u32[]{:S(2)}) copy-start(f32[2,1024]{1,0:T(2,128)} %param.10) | copy-start | bytes 24580
  46.6 148.5 %copy-start.1 = (f32[3,16]{1,0:T(4,128)S(1)}, f32[3,16]{1,0:T(4,128)}, u32[]{:S(2)}) copy-start(f32[3,16]{1,0:T(4,128)} %param.8) | copy-start | bytes 580
  46.6 148.5 %all-to-all-start = ((f32[64,3,4096]{2,1,0:T(4,128)}), f32[64,3,4096]{2,1,0:T(4,128)}, u32[]{:S(2)}, u32[]{:S(2)}) async-start(f32[64,3,4096]{2,1,0:T(4,128)} %stack.8), calls=%async_computation | async-start | bytes 8388608 | tf_op jit(solution)/shard_map/all_to_all | solution.py:50
  54.1 140.9 %all-gather.2.cloned.1.call-start = ((), (), s32[]{:S(2)}) async-start(), calls=%async_computation.2 | async-start | bytes 2129920 | tf_op jit(solution)/shard_map/all_gather | solution.py:52
Sparse Core Ops, SparseCore 0:
  66.1 128.9 all-gather.1
